TPU v7x, 32 devices: a whole 2x2x4 slice. The times are simulated.
32 devices in a mesh: groups: 2 (over x), chan: 16 (over z, y, core).
Axes of the slice: x: 2, y: 2, z: 4, core: 2. Of those that a mesh axis runs over, the one named last changes fastest.
Arguments:
- spectra: bfloat16 [2, 8, 512, 512], P(None, 'groups', 'chan'), parts along dimension 1, may hold values from -6 to 6
- filter_bank: float32 [2, 8, 65], replicated, may hold values from -0.5 to 0.5
- band_index: int32 [512], replicated, may hold values from 0 to 7
- window_mask: int32 [8, 512], P('groups', 'chan'), parts along dimension 0, may hold values 0 or 1
- owner_order: int32 [8], P('groups'), parts along dimension 0, may hold values from 0 to 15, as said below
- source_offset: int32 [8, 32], P('groups'), parts along dimension 0, may hold values from 0 to 31, each once within a row
Outputs:
- cross: bfloat16 [2, 256, 512, 512], P(None, 'groups', 'chan'), parts along dimension 1
There are 2 independent parts, one for each index of `groups`. A program takes and returns all parts, laid end to end along the dimension named above; an argument that names none is the same for every part. Nothing has to cross between parts.
Inputs may be any that keep to these rules, and one draw needn't show every extreme that they name: `owner_order`: 4 distinct device indices, below 16.
All inputs are finite; a program needn't handle non-finite values. No bound on the sum of `window_mask` on one device may be relied on, other than what follows from the above.
Results may differ from a plain program's by a relative error of at most 0.0057.
Values may be sent and summed in bfloat16 or wider, within the bound.
A program may use at most 192 MiB of HBM per device.

v0:
```python
import functools

import jax
import jax.numpy as jnp
from jax import lax
from jax.experimental import pallas as pl
from jax.experimental.pallas import tpu as pltpu
from jax.sharding import PartitionSpec as P

SMOOTH = 17
water_level = 0.05
bf16 = jnp.bfloat16
f32 = jnp.float32
LANES = 128
LAG = 4


def split(x):
    hi = x.astype(bf16)
    return hi, (x - hi.astype(f32)).astype(bf16)


def build_toeplitz(bank_ref, toep):
    _, nbank, ntap = bank_ref.shape
    chans = toep.shape[1] // (2 * nbank)
    for b in range(nbank):
        parts = []
        for p in range(2):
            row = jnp.concatenate(
                [bank_ref[p, b : b + 1, :], jnp.zeros((1, LANES - ntap), f32)], axis=1
            )
            full = jnp.broadcast_to(row, (chans, LANES))
            parts.append(split(pltpu.roll(full, 0, 1, stride=1, stride_axis=0)))
        at = b * 2 * chans
        for part in range(2):
            real, imag = parts[0][part], parts[1][part]
            toep[part, at : at + chans, :LANES] = real
            toep[part, at : at + chans, LANES:] = -imag
            toep[part, at + chans : at + 2 * chans, :LANES] = imag
            toep[part, at + chans : at + 2 * chans, LANES:] = real


def build_window(band):
    bins = band.shape[0]
    rows = lax.broadcasted_iota(jnp.int32, (bins, bins), 0)
    cols = lax.broadcasted_iota(jnp.int32, (bins, bins), 1)
    band[...] = (jnp.abs(rows - cols) <= SMOOTH // 2).astype(f32).astype(bf16)


def filter_window(nbank, w, x, toep, index_ref, filt, power):
    bins = filt.shape[2]
    chans = toep.shape[1] // (2 * nbank)
    tile = 256
    rows = slice(w * chans, (w + 1) * chans)
    for n in range(bins // tile):
        cut = slice(n * tile, (n + 1) * tile)
        here = x(cut)
        res = jnp.dot(toep[0], here, preferred_element_type=f32)
        res += jnp.dot(toep[1], here, preferred_element_type=f32)
        index = index_ref[:, cut]
        acc = res[: 2 * chans]
        for b in range(1, nbank):
            acc = jnp.where(index == b, res[2 * chans * b : 2 * chans * (b + 1)], acc)
        real, imag = acc[:chans], acc[chans:]
        filt[0, rows, cut] = real
        filt[1, rows, cut] = imag
        hi, lo = split(real * real + imag * imag)
        power[0, rows, cut] = hi
        power[1, rows, cut] = lo


def whiten_window(w, band, mask_ref, filt, power):
    chans = mask_ref.shape[1]
    rows = slice(w * chans, (w + 1) * chans)
    smooth = jnp.dot(power[0, rows], band[...], preferred_element_type=f32)
    smooth += jnp.dot(power[1, rows], band[...], preferred_element_type=f32)
    scale = lax.rsqrt(smooth * (1.0 / SMOOTH) + water_level)
    eye = lax.broadcasted_iota(jnp.int32, (chans, chans), 0) == lax.broadcasted_iota(
        jnp.int32, (chans, chans), 1
    )
    row = jnp.broadcast_to(mask_ref[w : w + 1, :].astype(f32), (chans, chans))
    valid = jnp.sum(jnp.where(eye, row, 0.0), axis=1, keepdims=True)
    scale = scale * valid
    return [(filt[p, rows] * scale).astype(bf16) for p in range(2)]


class Line:
    def __init__(self, pos, length, device_of, lag, refs):
        self.pos, self.length, self.device_of, self.lag = pos, length, device_of, lag
        self.own, self.out_r, self.out_l, self.in_r, self.in_l, self.sems = refs
        self.count = self.own.shape[0]

    def clear(self):
        @pl.when(self.pos == 0)
        def _():
            self.in_r[...] = jnp.zeros_like(self.in_r)

        @pl.when(self.pos == self.length - 1)
        def _():
            self.in_l[...] = jnp.zeros_like(self.in_l)

    def copy(self, way, k):
        out, into = (self.out_r, self.in_r) if way == 0 else (self.out_l, self.in_l)
        other = self.pos + 1 if way == 0 else self.pos - 1
        return pltpu.make_async_remote_copy(
            src_ref=out.at[k],
            dst_ref=into.at[k],
            send_sem=self.sems.at[way, 0, k],
            recv_sem=self.sems.at[way, 1, k],
            device_id={"chan": self.device_of(other)},
            device_id_type=pl.DeviceIdType.MESH,
        )

    def tick(self, t):
        for way in range(2):
            behind = self.pos if way == 0 else self.length - 1 - self.pos
            out, into = (self.out_r, self.in_r) if way == 0 else (self.out_l, self.in_l)
            k = t - self.lag * behind
            inside = jnp.logical_and(k >= 0, k < self.count)

            @pl.when(jnp.logical_and(inside, behind > 0))
            def _(way=way, k=k):
                self.copy(way, k).wait_recv()

            @pl.when(jnp.logical_and(inside, behind < self.length - 1))
            def _(way=way, k=k, out=out, into=into):
                out[k] = self.own[k] + into[k]
                self.copy(way, k).start()

    def result(self, k):
        return self.own[k] + self.in_r[k] + self.in_l[k]

    def drain(self):
        for way in range(2):
            behind = self.pos if way == 0 else self.length - 1 - self.pos

            @pl.when(behind < self.length - 1)
            def _(way=way):
                @pl.loop(0, self.count)
                def _(k):
                    self.copy(way, k).wait_send()


def front_kernel(
    rows,
    cols,
    owner_ref,
    own_ref,
    bank_ref,
    index_ref,
    mask_ref,
    out_ref,
    src_ref,
    halo,
    toep,
    band,
    filt,
    power,
    mine,
    beside,
    row_buf,
    done,
    gathered,
    halo_sems,
    beside_sems,
    row_sems,
    gather_sems,
):
    wins, chans = mask_ref.shape
    bins = own_ref.shape[3]
    parts = 2 * cols
    subs, piece = beside.shape[1], beside.shape[2]
    me = lax.axis_index("chan")
    size = rows * cols * 2
    core = me % 2
    place = me % (2 * cols)
    base = me - place
    row = me // (2 * cols)
    partner = me + 1 - 2 * core
    mesh_id = pl.DeviceIdType.MESH

    barrier = pltpu.get_barrier_semaphore()
    partners = [
        (me > 0, me - 1),
        (me < size - 1, me + 1),
        (row > 0, me - 2 * cols),
        (row < rows - 1, me + 2 * cols),
    ] + [(place != j, base + j) for j in range(2 * cols)]
    expected = jnp.int32(0)
    for there, who in partners:
        expected += there.astype(jnp.int32)

        @pl.when(there)
        def _(who=who):
            pl.semaphore_signal(barrier, inc=1, device_id={"chan": who}, device_id_type=mesh_id)

    pl.semaphore_wait(barrier, expected)

    def halo_copy(way, w):
        return pltpu.make_async_remote_copy(
            src_ref=own_ref.at[:, w],
            dst_ref=halo.at[way, :, w],
            send_sem=halo_sems.at[way, 0, w],
            recv_sem=halo_sems.at[way, 1, w],
            device_id={"chan": me + 1 - 2 * way},
            device_id_type=mesh_id,
        )

    order = list(range(wins))
    sends = (me < size - 1, me > 0)
    for w in order:
        for way in range(2):

            @pl.when(sends[way])
            def _(way=way, w=w):
                halo_copy(way, w).start()

    for way in range(2):

        @pl.when(jnp.logical_not(sends[1 - way]))
        def _(way=way):
            halo[way] = jnp.zeros_like(halo[way])

    line = Line(row, rows, lambda i: i * 2 * cols + place, LAG, (*row_buf, row_sems))
    line.clear()
    build_toeplitz(bank_ref, toep)
    build_window(band)

    def beside_copy(sender, j):
        return pltpu.make_async_remote_copy(
            src_ref=mine.at[pl.ds(j * subs, subs)],
            dst_ref=beside.at[sender],
            send_sem=beside_sems.at[0, j],
            recv_sem=beside_sems.at[1, sender],
            device_id={"chan": base + j},
            device_id_type=mesh_id,
        )

    blank = jnp.zeros((LANES - 3 * chans, bins), bf16)
    for w in order:
        for way in range(2):

            @pl.when(sends[1 - way])
            def _(way=way, w=w):
                halo_copy(way, w).wait_recv()

        def x(cut, w=w):
            stack = []
            for p in range(2):
                stack += [halo[0, p, w, :, cut], own_ref[p, w, :, cut], halo[1, p, w, :, cut]]
                stack += [blank[:, cut]]
            return jnp.concatenate(stack, axis=0)

        filter_window(bank_ref.shape[1], w, x, toep, index_ref, filt, power)
        white = whiten_window(w, band, mask_ref, filt, power)
        for p in range(2):
            out_ref[p, w] = white[p]
            for i in range(chans // piece):
                mine[(w * 2 + p) * (chans // piece) + i] = white[p][i * piece : (i + 1) * piece]
        for j in range(w * parts // wins, (w + 1) * parts // wins):

            @pl.when(place != j)
            def _(j=j):
                beside_copy(place, j).start()

    beside[place] = mine[pl.ds(place * subs, subs)]
    for j in range(parts):

        @pl.when(place != j)
        def _(j=j):
            beside_copy(j, j).wait_recv()

    count = line.count

    @pl.loop(0, count)
    def _(k):
        total = jnp.zeros((piece, bins), bf16)
        for j in range(parts):
            total += beside[j, k % subs] * (owner_ref[k // subs] == base + j).astype(f32).astype(bf16)
        line.own[k] = total

    def give(src, origin, k, sem, who):
        return pltpu.make_async_remote_copy(
            src_ref=src,
            dst_ref=gathered.at[origin, k],
            send_sem=gather_sems.at[sem, k],
            recv_sem=gather_sems.at[2 * parts + origin, k],
            device_id={"chan": who},
            device_id_type=mesh_id,
        )

    def put(j, k, value):
        src_ref[k // subs, j * subs + k % subs] = value

    alike = [jnp.logical_and(place != j, core == j % 2) for j in range(parts)]
    last = LAG * (rows - 1)

    @pl.loop(0, count + last + LAG)
    def _(t):
        line.tick(t)
        k = t - last

        @pl.when(jnp.logical_and(k >= 0, k < count))
        def _():
            total = line.result(k)
            done[k] = total
            for j in range(parts):

                @pl.when(alike[j])
                def _(j=j):
                    give(done.at[k], place, k, j, base + j).start()

            give(done.at[k], place, k, parts + place, partner).start()
            put(place, k, total)

        q = t - last - LAG

        @pl.when(q >= 0)
        def _():
            for j in range(parts):

                @pl.when(alike[j])
                def _(j=j):
                    give(done.at[q], j, q, j, partner).wait_recv()
                    give(gathered.at[j, q], j, q, parts + j, partner).start()
                    put(j, q, gathered[j, q])

    @pl.loop(0, count)
    def _(k):
        for j in range(parts):

            @pl.when(core != j % 2)
            def _(j=j):
                give(done.at[k], j, k, j, partner).wait_recv()
                put(j, k, gathered[j, k])

    for way in range(2):
        for w in range(wins):

            @pl.when(sends[way])
            def _(way=way, w=w):
                halo_copy(way, w).wait_send()

    for j in range(parts):

        @pl.when(place != j)
        def _(j=j):
            beside_copy(place, j).wait_send()

    line.drain()

    @pl.loop(0, count)
    def _(k):
        give(done.at[k], place, k, parts + place, partner).wait_send()
        for j in range(parts):

            @pl.when(alike[j])
            def _(j=j):
                give(done.at[k], place, k, j, partner).wait_send()
                give(gathered.at[j, k], j, k, parts + j, partner).wait_send()


def front(grid, owner, own, bank, index, mask):
    _, wins, chans, bins = own.shape
    nbank = bank.shape[1]
    rounds = owner.shape[0]
    rows, cols = grid
    parts = 2 * cols
    total = wins * 2 * chans
    piece = min(chans, total // parts)
    subs = total // parts // piece
    count = rounds * subs
    vmem = pl.BlockSpec(memory_space=pltpu.VMEM)
    chunk = (piece, bins)
    chunks = pltpu.VMEM((count, *chunk), bf16)
    return pl.pallas_call(
        functools.partial(front_kernel, rows, cols),
        out_shape=[
            jax.ShapeDtypeStruct(own.shape, bf16),
            jax.ShapeDtypeStruct((rounds, parts * subs, piece, bins), bf16),
        ],
        in_specs=[pl.BlockSpec(memory_space=pltpu.SMEM)] + [vmem] * 4,
        out_specs=[vmem] * 2,
        scratch_shapes=[
            pltpu.VMEM((2, *own.shape), bf16),
            pltpu.VMEM((2, nbank * 2 * chans, 2 * LANES), bf16),
            pltpu.VMEM((bins, bins), bf16),
            pltpu.VMEM((2, wins * chans, bins), f32),
            pltpu.VMEM((2, wins * chans, bins), bf16),
            pltpu.VMEM((parts * subs, *chunk), bf16),
            pltpu.VMEM((parts, subs, *chunk), bf16),
            [chunks] * 5,
            chunks,
            pltpu.VMEM((parts, count, *chunk), bf16),
            pltpu.SemaphoreType.DMA((2, 2, wins)),
            pltpu.SemaphoreType.DMA((2, parts)),
            pltpu.SemaphoreType.DMA((2, 2, count)),
            pltpu.SemaphoreType.DMA((3 * parts, count)),
        ],
        compiler_params=pltpu.CompilerParams(collective_id=0, has_side_effects=True),
        name="front",
    )(owner, own, bank, index, mask)


def tree_sum(terms):
    while len(terms) > 1:
        terms = [a + b for a, b in zip(terms[::2], terms[1::2])]
    return terms[0]


def cross_kernel(offset_ref, src_ref, loc_ref, out_ref, wide, held):
    _, wins, chans, bins = loc_ref.shape
    count = out_ref.shape[1]
    r, h = pl.program_id(0), pl.program_id(1)

    @pl.when(jnp.logical_and(r == 0, h == 0))
    def _():
        held[...] = loc_ref[...]

    @pl.when(h == 0)
    def _():
        for p in range(2):
            for w in range(wins):
                wide[:, p * wins + w, :] = src_ref[0, w, p].astype(f32) * (1.0 / wins)

    for n in range(bins // LANES):
        cut = slice(n * LANES, (n + 1) * LANES)

        def one(j, carry, cut=cut):
            loc = [[held[p, w, :, cut] for w in range(wins)] for p in range(2)]
            at = offset_ref[r, h * count + j]
            src = [
                [
                    jnp.broadcast_to(
                        wide[at, p * wins + w : p * wins + w + 1, cut], (chans, LANES)
                    ).astype(bf16)
                    for w in range(wins)
                ]
                for p in range(2)
            ]
            real = tree_sum(
                [src[p][w] * loc[p][w] for w in range(wins) for p in range(2)]
            )
            plus = tree_sum([src[0][w] * loc[1][w] for w in range(wins)])
            minus = tree_sum([src[1][w] * loc[0][w] for w in range(wins)])
            out_ref[0, j, :, cut] = real
            out_ref[1, j, :, cut] = plus - minus
            return carry

        lax.fori_loop(0, count, one, 0, unroll=4)


def cross(offset, src, loc, blocks=1):
    rounds, wins, _, chans, bins = src.shape
    per = chans // blocks
    return pl.pallas_call(
        cross_kernel,
        out_shape=jax.ShapeDtypeStruct((2, rounds * chans, chans, bins), bf16),
        grid=(rounds, blocks),
        in_specs=[
            pl.BlockSpec(memory_space=pltpu.SMEM),
            pl.BlockSpec((1, wins, 2, chans, bins), lambda r, h: (r, 0, 0, 0, 0)),
            pl.BlockSpec((2, wins, chans, bins), lambda r, h: (0, 0, 0, 0)),
        ],
        out_specs=pl.BlockSpec((2, per, chans, bins), lambda r, h: (0, r * blocks + h, 0, 0)),
        scratch_shapes=[
            pltpu.VMEM((chans, 2 * wins, bins), f32),
            pltpu.VMEM((2, wins, chans, bins), bf16),
        ],
        name="cross",
    )(offset, src, loc)


def chip_grid(size):
    chips = size // 2
    cols = 1
    while cols * cols * 4 <= chips:
        cols *= 2
    return chips // cols, cols


def body(spectra, filter_bank, band_index, window_mask, owner_order, source_offset):
    grid = chip_grid(lax.axis_size("chan"))
    whitened, sources = front(
        grid, owner_order, spectra, filter_bank, band_index[None, :], window_mask
    )
    _, wins, chans, bins = spectra.shape
    sources = sources.reshape(sources.shape[0], wins, 2, chans, bins)
    return cross(source_offset, sources, whitened)


def solution(mesh):
    in_specs = (
        P(None, "groups", "chan", None),
        P(),
        P(),
        P("groups", "chan"),
        P("groups"),
        P("groups", None),
    )
    out_specs = P(None, "groups", "chan", None)
    return jax.shard_map(body, mesh=mesh, in_specs=in_specs, out_specs=out_specs, check_vma=False)
```

profile of v0, /device:TPU:0, one launch (start us, length us, event | category | flops | bytes accessed | tf_op | source)
XLA Modules:
  0.0 47.5 jit_solution(10680898248450791268)
XLA Ops:
  0.0 37.5 %front.1 = (bf16[2,4,32,512]{3,2,1,0:T(8,128)(2,1)}, bf16[4,8,32,512]{3,2,1,0:T(8,128)(2,1)}) custom-call(s32[4]{0:T(128)} %owner_ref.1, bf16[2,4,32,512]{3,2,1,0:T(8,128)(2,1)} %own_ref.1, f32[2,8,65]{2,1,0:T(8,128)} %bank_ref.1, s32[1,512]{1,0:T(1,128)} %bitcast.3, s32[4,32]{1,0:T(4,128)} %mask_ref.1), custom_call_target="tpu_custom_call" | custom-call | tf_op jit(solution)/shard_map/front/pallas_call | solution.py:376
  37.5 10.0 %cross.1 = bf16[2,128,32,512]{3,2,1,0:T(8,128)(2,1)} custom-call(s32[4,32]{1,0:T(4,128)} %offset_ref.1, bf16[4,4,2,32,512]{4,3,2,1,0:T(8,128)(2,1)} %bitcast.2, bf16[2,4,32,512]{3,2,1,0:T(8,128)(2,1)} %get-tuple-element.8.loc_ref), custom_call_target="tpu_custom_call" | custom-call | tf_op jit(solution)/shard_map/cross/pallas_call | solution.py:456
where the time goes:
time: 47.8 us; the launch traced here: 47.5 us
  Pallas kernels  47.5 us (99%)
    pallas_call x1, Pallas kernels, front(): pl.pallas_call(functools.partial(front_kernel, rows, cols), out_shape=[ja...  37.5 us
    pallas_call x1, Pallas kernels, cross(): pl.pallas_call(cross_kernel, out_shape=jax.ShapeDtypeStruct((2, rounds *...  9.99 us

commit v1 on v0

--- a/solution.py
+++ b/solution.py
@@ -479,12 +479,501 @@
     return chips // cols, cols
 
 
+HOP = 6
+
+
+def build_bank(bank_ref, toep):
+    _, nbank, ntap = bank_ref.shape
+    outs = toep.shape[1] // (2 * nbank)
+    for b in range(nbank):
+        parts = []
+        for p in range(2):
+            row = jnp.concatenate(
+                [bank_ref[p, b : b + 1, :], jnp.zeros((1, LANES - ntap), f32)], axis=1
+            )
+            full = jnp.broadcast_to(row, (outs, LANES))
+            parts.append(split(pltpu.roll(full, 0, 1, stride=1, stride_axis=0)))
+        at = b * 2 * outs
+        for part in range(2):
+            real, imag = parts[0][part], parts[1][part]
+            toep[part, at : at + outs, :LANES] = real
+            toep[part, at : at + outs, LANES:] = -imag
+            toep[part, at + outs : at + 2 * outs, :LANES] = imag
+            toep[part, at + outs : at + 2 * outs, LANES:] = real
+
+
+def build_band(band):
+    wide, bins = band.shape
+    rows = lax.broadcasted_iota(jnp.int32, (wide, bins), 0)
+    cols = lax.broadcasted_iota(jnp.int32, (wide, bins), 1)
+    band[...] = (jnp.abs(rows - bins - cols) <= SMOOTH // 2).astype(f32).astype(bf16)
+
+
+def build_pick(base, place, owner_ref, offset_ref, masks, pick):
+    parts, _, chans = masks.shape
+    rounds = offset_ref.shape[0]
+    total = parts * chans
+    valid = jnp.concatenate(
+        [masks[b, pl.ds(place, 1), :].astype(f32) for b in range(parts)], axis=1
+    )
+    eye = lax.broadcasted_iota(jnp.int32, (chans, chans), 0) == lax.broadcasted_iota(
+        jnp.int32, (chans, chans), 1
+    )
+    cols = lax.broadcasted_iota(jnp.int32, (chans, total), 1).astype(f32)
+    for r in range(rounds):
+        row = jnp.broadcast_to(offset_ref[r : r + 1, :].astype(f32), (chans, chans))
+        col = jnp.sum(jnp.where(eye, row, 0.0), axis=1, keepdims=True)
+        col = col + ((owner_ref[r] - base) * chans).astype(f32)
+        pick[r * chans : (r + 1) * chans] = jnp.where(cols == col, valid, 0.0).astype(bf16)
+    rows = lax.broadcasted_iota(jnp.int32, (total, total), 0)
+    same = rows == lax.broadcasted_iota(jnp.int32, (total, total), 1)
+    pick[rounds * chans :] = jnp.where(same, valid, 0.0).astype(bf16)
+
+
+def filter_cut(q, nbank, raw, toep, index_ref, filt, power):
+    outs = toep.shape[1] // (2 * nbank)
+    blocks, chans = raw.shape[1], raw.shape[3]
+    step = outs // chans
+    index = index_ref[:, q * LANES : (q + 1) * LANES]
+    for u in range((blocks - 2) // step):
+        here = [
+            raw[q, u * step : u * step + step + 2, p].reshape((step + 2) * chans, LANES)
+            for p in range(2)
+        ]
+        here = jnp.concatenate(here, axis=0)
+        res = jnp.dot(toep[0], here, preferred_element_type=f32)
+        res += jnp.dot(toep[1], here, preferred_element_type=f32)
+        acc = res[: 2 * outs]
+        for b in range(1, nbank):
+            acc = jnp.where(index == b, res[2 * outs * b : 2 * outs * (b + 1)], acc)
+        real, imag = acc[:outs], acc[outs:]
+        rows = slice(u * outs, (u + 1) * outs)
+        filt[q, 0, rows] = real
+        filt[q, 1, rows] = imag
+        power[rows, (q + 1) * LANES : (q + 2) * LANES] = (real * real + imag * imag).astype(bf16)
+
+
+def whiten_cut(q, band, pick, filt, power, own, mine):
+    rounds = own.shape[0] // filt.shape[0]
+    chans = own.shape[2]
+    smooth = jnp.dot(
+        power[:, q * LANES : (q + 3) * LANES], band[...], preferred_element_type=f32
+    )
+    scale = lax.rsqrt(smooth * (1.0 / SMOOTH) + water_level)
+    for p in range(2):
+        white = (filt[q, p] * scale).astype(bf16)
+        res = jnp.dot(pick[...], white, preferred_element_type=f32).astype(bf16)
+        for r in range(rounds):
+            own[q * rounds + r, p] = res[r * chans : (r + 1) * chans]
+        at = rounds * chans
+        for b in range(mine.shape[1]):
+            mine[q, b, p] = res[at + b * chans : at + (b + 1) * chans]
+
+
+def row_kernel(
+    rows,
+    owner_in,
+    own_in,
+    bank_in,
+    index_in,
+    mask_in,
+    offset_in,
+    loc_ref,
+    src_ref,
+    owner_ref,
+    own_ref,
+    bank_ref,
+    index_ref,
+    mask_ref,
+    offset_ref,
+    in_sems,
+    raw,
+    masks,
+    toep,
+    band,
+    pick,
+    filt,
+    power,
+    mine,
+    back,
+    line_buf,
+    done,
+    across,
+    beside,
+    raw_send,
+    raw_recv,
+    mask_sems,
+    back_sems,
+    line_sems,
+    give_sems,
+):
+    wins, chans = mask_ref.shape
+    cuts = raw.shape[0]
+    nbank = bank_ref.shape[1]
+    parts = wins
+    rounds = owner_ref.shape[0]
+    me = lax.axis_index("chan")
+    core = me % 2
+    place = me % parts
+    base = me - place
+    row = me // parts
+    partner = me + 1 - 2 * core
+    alike = base + (place + 2) % parts
+    partner_place = place + 1 - 2 * core
+    alike_place = (place + 2) % parts
+    corner_place = (partner_place + 2) % parts
+    mesh_id = pl.DeviceIdType.MESH
+
+    def send(src, dst, send_sem, recv_sem, who):
+        return pltpu.make_async_remote_copy(
+            src_ref=src,
+            dst_ref=dst,
+            send_sem=send_sem,
+            recv_sem=recv_sem,
+            device_id={"chan": who},
+            device_id_type=mesh_id,
+        )
+
+    pairs_in = [
+        (own_in, own_ref),
+        (mask_in, mask_ref),
+        (bank_in, bank_ref),
+        (index_in, index_ref),
+        (offset_in, offset_ref),
+        (owner_in, owner_ref),
+    ]
+    inputs = [
+        pltpu.make_async_copy(src, dst, in_sems.at[n]) for n, (src, dst) in enumerate(pairs_in)
+    ]
+    for copy in inputs:
+        copy.start()
+
+    barrier = pltpu.get_barrier_semaphore()
+    partners = [(place != j, base + j) for j in range(parts)]
+    for j in range(parts):
+        near = jnp.logical_or(place == j, jnp.logical_or(place == parts - 1, j == 0))
+        partners.append((jnp.logical_and(row < rows - 1, near), base + parts + j))
+        near = jnp.logical_or(place == j, jnp.logical_or(place == 0, j == parts - 1))
+        partners.append((jnp.logical_and(row > 0, near), base - parts + j))
+    expected = jnp.int32(0)
+    for there, who in partners:
+        expected += there.astype(jnp.int32)
+
+        @pl.when(there)
+        def _(who=who):
+            pl.semaphore_signal(barrier, inc=1, device_id={"chan": who}, device_id_type=mesh_id)
+
+    pl.semaphore_wait(barrier, expected)
+
+    peers = [alike_place, corner_place, partner_place]
+
+    def raw_copy(q, to, slot, n, who):
+        return send(
+            own_ref.at[:, to, :, q * LANES : (q + 1) * LANES],
+            raw.at[q, slot],
+            raw_send.at[q, n],
+            raw_recv.at[q, slot],
+            who,
+        )
+
+    def mask_copy(n):
+        return send(
+            mask_ref, masks.at[place], mask_sems.at[0, n], mask_sems.at[1, place], base + peers[n]
+        )
+
+    above = jnp.logical_and(place == parts - 1, row < rows - 1)
+    below = jnp.logical_and(place == 0, row > 0)
+
+    def edges(q, act):
+        @pl.when(above)
+        def _():
+            for j in range(parts):
+                act(raw_copy(q, j, 0, parts - 1 + j, base + parts + j))
+
+        @pl.when(below)
+        def _():
+            for j in range(parts):
+                act(raw_copy(q, j, parts + 1, parts - 1 + j, base - parts + j))
+
+    for copy in inputs:
+        copy.wait()
+    for n in range(parts - 1):
+        mask_copy(n).start()
+    for q in range(cuts):
+        for n in range(2):
+            raw_copy(q, peers[n], 1 + place, n, base + peers[n]).start()
+        edges(q, lambda copy: copy.start())
+        raw_copy(q, peers[2], 1 + place, 2, base + peers[2]).start()
+
+    masks[place] = mask_ref[...]
+    for q in range(cuts):
+        raw[q, 1 + place] = own_ref[:, place, :, q * LANES : (q + 1) * LANES]
+
+    @pl.when(row == 0)
+    def _():
+        raw[:, 0] = jnp.zeros_like(raw[:, 0])
+
+    @pl.when(row == rows - 1)
+    def _():
+        raw[:, parts + 1] = jnp.zeros_like(raw[:, parts + 1])
+
+    line = Line(row, rows, lambda i: i * parts + place, HOP, (*line_buf, line_sems))
+    line.clear()
+    build_bank(bank_ref, toep)
+    build_band(band)
+    edge = jnp.zeros((power.shape[0], LANES), bf16)
+    power[:, :LANES] = edge
+    power[:, (cuts + 1) * LANES :] = edge
+
+    for b in range(parts):
+
+        @pl.when(place != b)
+        def _(b=b):
+            send(mask_ref, masks.at[b], mask_sems.at[0, 0], mask_sems.at[1, b], partner).wait_recv()
+
+    build_pick(base, place, owner_ref, offset_ref, masks, pick)
+
+    count = line.count
+    last = HOP * (rows - 1)
+
+    def give(src, dst, n, k, who):
+        return send(src.at[k], dst.at[k], give_sems.at[0, n, k], give_sems.at[1, n, k], who)
+
+    def put(k, j, value):
+        src_ref[k, j] = value.astype(f32) * (1.0 / wins)
+
+    def tick(t):
+        line.tick(t)
+        k = t - last
+
+        @pl.when(jnp.logical_and(k >= 0, k < count))
+        def _():
+            total = line.result(k)
+            done[k] = total
+            give(done, across, 0, k, alike).start()
+            give(done, beside.at[0], 1, k, partner).start()
+            put(k, place, total)
+
+        q = t - last - HOP
+
+        @pl.when(jnp.logical_and(q >= 0, q < count))
+        def _():
+            give(done, across, 0, q, alike).wait_recv()
+            give(across, beside.at[1], 2, q, partner).start()
+            put(q, alike_place, across[q])
+
+        b = t - last - 2 * HOP
+
+        @pl.when(jnp.logical_and(b >= 0, b < count))
+        def _():
+            give(done, beside.at[0], 1, b, partner).wait_recv()
+            put(b, partner_place, beside[0, b])
+            give(across, beside.at[1], 2, b, partner).wait_recv()
+            put(b, corner_place, beside[1, b])
+
+    def back_copy(q, n):
+        return send(
+            mine.at[q, peers[n]],
+            back.at[q, place],
+            back_sems.at[0, q, n],
+            back_sems.at[1, q, place],
+            base + peers[n],
+        )
+
+    def finish(q):
+        whiten_cut(q, band, pick, filt, power, line.own, mine)
+        back[q, place] = mine[q, place]
+
+        @pl.loop(q * rounds, (q + 1) * rounds)
+        def _(t):
+            tick(t)
+
+        for n in range(parts - 1):
+            back_copy(q, n).start()
+
+    for q in range(cuts):
+        for slot in range(parts + 2):
+            there = place != slot - 1
+            if slot == 0:
+                there = row > 0
+            if slot == parts + 1:
+                there = row < rows - 1
+
+            @pl.when(there)
+            def _(slot=slot, q=q):
+                raw_copy(q, 0, slot, 0, partner).wait_recv()
+
+        filter_cut(q, nbank, raw, toep, index_ref, filt, power)
+        if q > 0:
+            finish(q - 1)
+    finish(cuts - 1)
+
+    @pl.loop(cuts * rounds, count + last + 2 * HOP)
+    def _(t):
+        tick(t)
+
+    for q in range(cuts):
+        for n in range(parts - 1):
+            j = peers[n]
+            send(
+                mine.at[q, 0], back.at[q, j], back_sems.at[0, q, n], back_sems.at[1, q, j], partner
+            ).wait_recv()
+    loc_ref[...] = back[...]
+
+    for n in range(parts - 1):
+        mask_copy(n).wait_send()
+    for q in range(cuts):
+        for n in range(parts - 1):
+            raw_copy(q, peers[n], 1 + place, n, base + peers[n]).wait_send()
+            back_copy(q, n).wait_send()
+        edges(q, lambda copy: copy.wait_send())
+    line.drain()
+
+    @pl.loop(0, count)
+    def _(k):
+        give(done, across, 0, k, alike).wait_send()
+        give(done, beside.at[0], 1, k, partner).wait_send()
+        give(across, beside.at[1], 2, k, partner).wait_send()
+
+
+def row_front(rows, owner, own, bank, index, mask, offset):
+    _, wins, chans, bins = own.shape
+    nbank = bank.shape[1]
+    rounds = owner.shape[0]
+    cuts = bins // LANES
+    parts = wins
+    count = cuts * rounds
+    outs = LANES // 2
+    vmem = pl.BlockSpec(memory_space=pltpu.VMEM)
+    chunk = (2, chans, LANES)
+    chunks = pltpu.VMEM((count, *chunk), bf16)
+    return pl.pallas_call(
+        functools.partial(row_kernel, rows),
+        out_shape=[
+            jax.ShapeDtypeStruct((cuts, wins, *chunk), bf16),
+            jax.ShapeDtypeStruct((count, wins, *chunk), f32),
+        ],
+        in_specs=[pl.BlockSpec(memory_space=pltpu.HBM)] * 6,
+        out_specs=[vmem] * 2,
+        scratch_shapes=[
+            pltpu.SMEM(owner.shape, owner.dtype),
+            *[pltpu.VMEM(a.shape, a.dtype) for a in (own, bank, index, mask, offset)],
+            pltpu.SemaphoreType.DMA((6,)),
+            pltpu.VMEM((cuts, parts + 2, *chunk), bf16),
+            pltpu.VMEM((parts, wins, chans), jnp.int32),
+            pltpu.VMEM((2, nbank * 2 * outs, 2 * LANES), bf16),
+            pltpu.VMEM((3 * LANES, LANES), bf16),
+            pltpu.VMEM(((rounds + parts) * chans, parts * chans), bf16),
+            pltpu.VMEM((cuts, 2, parts * chans, LANES), f32),
+            pltpu.VMEM((parts * chans, (cuts + 2) * LANES), bf16),
+            pltpu.VMEM((cuts, parts, *chunk), bf16),
+            pltpu.VMEM((cuts, parts, *chunk), bf16),
+            [chunks] * 5,
+            chunks,
+            chunks,
+            pltpu.VMEM((2, count, *chunk), bf16),
+            pltpu.SemaphoreType.DMA((cuts, 2 * parts - 1)),
+            pltpu.SemaphoreType.DMA((cuts, parts + 2)),
+            pltpu.SemaphoreType.DMA((2, parts)),
+            pltpu.SemaphoreType.DMA((2, cuts, parts)),
+            pltpu.SemaphoreType.DMA((2, 2, count)),
+            pltpu.SemaphoreType.DMA((2, 3, count)),
+        ],
+        compiler_params=pltpu.CompilerParams(
+            collective_id=0, has_side_effects=True, vmem_limit_bytes=24 << 20
+        ),
+        name="front",
+    )(*[pltpu.with_memory_space_constraint(a, pltpu.HBM) for a in (owner, own, bank, index, mask, offset)])
+
+
+def pairs_kernel(src_ref, loc_ref, out_ref, buf, sems):
+    cuts, wins, _, chans, _ = loc_ref.shape
+    slots, _, per = buf.shape[:3]
+    rounds = src_ref.shape[0] // cuts
+    steps = rounds * chans // per
+
+    def flush(step):
+        slot = step % slots
+        return pltpu.make_async_copy(
+            buf.at[slot], out_ref.at[:, pl.ds(step * per, per)], sems.at[slot]
+        )
+
+    @pl.loop(0, steps)
+    def _(step):
+        slot = step % slots
+        r = step * per // chans
+        first = step * per % chans
+
+        @pl.when(step >= slots)
+        def _():
+            flush(step - slots).wait()
+
+        for q in range(cuts):
+            loc = [[loc_ref[q, w, p] for w in range(wins)] for p in range(2)]
+
+            def one(j, carry, q=q, loc=loc):
+                src = [
+                    [
+                        jnp.broadcast_to(
+                            src_ref[q * rounds + r, w, p, pl.ds(first + j, 1), :], (chans, LANES)
+                        ).astype(bf16)
+                        for w in range(wins)
+                    ]
+                    for p in range(2)
+                ]
+                real = tree_sum([src[p][w] * loc[p][w] for w in range(wins) for p in range(2)])
+                plus = tree_sum([src[0][w] * loc[1][w] for w in range(wins)])
+                minus = tree_sum([src[1][w] * loc[0][w] for w in range(wins)])
+                cut = slice(q * LANES, (q + 1) * LANES)
+                buf[slot, 0, j, :, cut] = real
+                buf[slot, 1, j, :, cut] = plus - minus
+                return carry
+
+            lax.fori_loop(0, per, one, 0, unroll=8)
+        flush(step).start()
+
+    for n in range(slots):
+        flush(steps - slots + n).wait()
+
+
+def pairs(src, loc):
+    cuts, wins, _, chans, _ = loc.shape
+    count = src.shape[0] // cuts * chans
+    per = chans // 2
+    slots = 2
+    vmem = pl.BlockSpec(memory_space=pltpu.VMEM)
+    return pl.pallas_call(
+        pairs_kernel,
+        out_shape=jax.ShapeDtypeStruct((2, count, chans, cuts * LANES), bf16),
+        in_specs=[vmem] * 2,
+        out_specs=pl.BlockSpec(memory_space=pl.ANY),
+        scratch_shapes=[
+            pltpu.VMEM((slots, 2, per, chans, cuts * LANES), bf16),
+            pltpu.SemaphoreType.DMA((slots,)),
+        ],
+        compiler_params=pltpu.CompilerParams(vmem_limit_bytes=16 << 20),
+        name="pairs",
+    )(src, loc)
+
+
 def body(spectra, filter_bank, band_index, window_mask, owner_order, source_offset):
     grid = chip_grid(lax.axis_size("chan"))
+    _, wins, chans, bins = spectra.shape
+    ntap = filter_bank.shape[2]
+    if 2 * grid[1] == wins == 4 and 4 * chans == LANES and ntap == 2 * chans + 1:
+        whitened, sources = row_front(
+            grid[0],
+            owner_order,
+            spectra,
+            filter_bank,
+            band_index[None, :],
+            window_mask,
+            source_offset,
+        )
+        return pairs(sources, whitened)
     whitened, sources = front(
         grid, owner_order, spectra, filter_bank, band_index[None, :], window_mask
     )
-    _, wins, chans, bins = spectra.shape
     sources = sources.reshape(sources.shape[0], wins, 2, chans, bins)
     return cross(source_offset, sources, whitened)
 

time: 47.8 us -> 39.3 us (0.82)
  Pallas kernels: 47.5 us -> 39 us
    pallas_call x2, Pallas kernels: 47.5 us -> 39 us  [the longest x1 31.3 us: row_front(): pl.pallas_call(functools.partial(row_kernel, rows), out_shape=[jax.ShapeD...]
where the time goes in v1:
time: 39.3 us; the launch traced here: 39 us
  Pallas kernels  39 us (99%)
    pallas_call x1, Pallas kernels, row_front(): pl.pallas_call(functools.partial(row_kernel, rows), out_shape=[jax.ShapeD...  31.3 us
    pallas_call x1, Pallas kernels, pairs(): pl.pallas_call(pairs_kernel, out_shape=jax.ShapeDtypeStruct((2, count, ch...  7.71 us

profile of v1, /device:TPU:0, one launch (start us, length us, event | category | flops | bytes accessed | tf_op | source)
XLA Modules:
  0.0 39.0 jit_solution(7018741561878350933)
XLA Ops:
  0.0 31.3 %front.1 = (bf16[4,4,2,32,128]{4,3,2,1,0:T(8,128)(2,1)S(1)}, f32[16,4,2,32,128]{4,3,2,1,0:T(8,128)S(1)}) custom-call(s32[4]{0:T(128)} %owner_in.1, bf16[2,4,32,512]{3,2,1,0:T(8,128)(2,1)} %own_in.1, f32[2,8,65]{2,1,0:T(8,128)} %bank_in.1, s32[1,512]{1,0:T(1,128)} %bitcast.1, s32[4,32]{1,0:T(4,128)} %mask_in.1, s32[4,32]{1,0:T(4,128)} %offset_in.1), custom_call_target="tpu_custom_call" | custom-call | tf_op jit(solution)/shard_map/front/pallas_call | solution.py:850
  31.3 7.7 %pairs.1 = bf16[2,128,32,512]{3,2,1,0:T(8,128)(2,1)} custom-call(f32[16,4,2,32,128]{4,3,2,1,0:T(8,128)S(1)} %get-tuple-element.7.src_ref, bf16[4,4,2,32,128]{4,3,2,1,0:T(8,128)(2,1)S(1)} %get-tuple-element.8.loc_ref), custom_call_target="tpu_custom_call" | custom-call | tf_op jit(solution)/shard_map/pairs/pallas_call | solution.py:945

commit v2 on v1

--- a/solution.py
+++ b/solution.py
@@ -479,12 +479,38 @@
     return chips // cols, cols
 
 
-HOP = 6
+HOP, SIDE, NEAR = 10, 8, 4
+
+
+class Chain(Line):
+    def copy(self, way, k):
+        out, into = (self.out_r, self.in_r) if way == 0 else (self.out_l, self.in_l)
+        other = self.pos + 1 if way == 0 else self.pos - 1
+        return self.make(way, out.at[k], into.at[k], k, self.device_of(other))
+
+    def make(self, way, src, dst, k, who):
+        return pltpu.make_async_remote_copy(
+            src_ref=src,
+            dst_ref=dst,
+            send_sem=self.sems.at[way, self.count],
+            recv_sem=self.sems.at[way, k],
+            device_id={"chan": who},
+            device_id_type=pl.DeviceIdType.MESH,
+        )
+
+    def drain(self, who):
+        for way in range(2):
+            behind = self.pos if way == 0 else self.length - 1 - self.pos
+            out = self.out_r if way == 0 else self.out_l
+
+            @pl.when(behind < self.length - 1)
+            def _(way=way, out=out):
+                self.make(way, out, out, 0, who).wait_send()
 
 
 def build_bank(bank_ref, toep):
     _, nbank, ntap = bank_ref.shape
-    outs = toep.shape[1] // (2 * nbank)
+    outs = toep.shape[0] // (2 * nbank)
     for b in range(nbank):
         parts = []
         for p in range(2):
@@ -496,10 +522,12 @@
         at = b * 2 * outs
         for part in range(2):
             real, imag = parts[0][part], parts[1][part]
-            toep[part, at : at + outs, :LANES] = real
-            toep[part, at : at + outs, LANES:] = -imag
-            toep[part, at + outs : at + 2 * outs, :LANES] = imag
-            toep[part, at + outs : at + 2 * outs, LANES:] = real
+            left = slice(2 * part * LANES, (2 * part + 1) * LANES)
+            right = slice((2 * part + 1) * LANES, (2 * part + 2) * LANES)
+            toep[at : at + outs, left] = real
+            toep[at : at + outs, right] = -imag
+            toep[at + outs : at + 2 * outs, left] = imag
+            toep[at + outs : at + 2 * outs, right] = real
 
 
 def build_band(band):
@@ -530,27 +558,38 @@
     pick[rounds * chans :] = jnp.where(same, valid, 0.0).astype(bf16)
 
 
-def filter_cut(q, nbank, raw, toep, index_ref, filt, power):
-    outs = toep.shape[1] // (2 * nbank)
+def filter_cuts(first, cuts, nbank, raw, toep, index_ref, filt, power):
+    outs = toep.shape[0] // (2 * nbank)
     blocks, chans = raw.shape[1], raw.shape[3]
     step = outs // chans
-    index = index_ref[:, q * LANES : (q + 1) * LANES]
+    many = range(first, first + cuts)
+    index = index_ref[:, first * LANES : (first + cuts) * LANES]
     for u in range((blocks - 2) // step):
         here = [
-            raw[q, u * step : u * step + step + 2, p].reshape((step + 2) * chans, LANES)
+            jnp.concatenate(
+                [
+                    raw[q, u * step : u * step + step + 2, p].reshape((step + 2) * chans, LANES)
+                    for q in many
+                ],
+                axis=1,
+            )
             for p in range(2)
         ]
-        here = jnp.concatenate(here, axis=0)
-        res = jnp.dot(toep[0], here, preferred_element_type=f32)
-        res += jnp.dot(toep[1], here, preferred_element_type=f32)
+        res = jnp.dot(
+            toep[...], jnp.concatenate(here + here, axis=0), preferred_element_type=f32
+        )
         acc = res[: 2 * outs]
         for b in range(1, nbank):
             acc = jnp.where(index == b, res[2 * outs * b : 2 * outs * (b + 1)], acc)
         real, imag = acc[:outs], acc[outs:]
         rows = slice(u * outs, (u + 1) * outs)
-        filt[q, 0, rows] = real
-        filt[q, 1, rows] = imag
-        power[rows, (q + 1) * LANES : (q + 2) * LANES] = (real * real + imag * imag).astype(bf16)
+        for q in many:
+            cut = slice((q - first) * LANES, (q - first + 1) * LANES)
+            filt[q, 0, rows] = real[:, cut]
+            filt[q, 1, rows] = imag[:, cut]
+        power[rows, (first + 1) * LANES : (first + cuts + 1) * LANES] = (
+            real * real + imag * imag
+        ).astype(bf16)
 
 
 def whiten_cut(q, band, pick, filt, power, own, mine):
@@ -580,6 +619,7 @@
     offset_in,
     loc_ref,
     src_ref,
+    part_ref,
     owner_ref,
     own_ref,
     bank_ref,
@@ -606,6 +646,7 @@
     back_sems,
     line_sems,
     give_sems,
+    give_recv,
 ):
     wins, chans = mask_ref.shape
     cuts = raw.shape[0]
@@ -671,14 +712,14 @@
         return send(
             own_ref.at[:, to, :, q * LANES : (q + 1) * LANES],
             raw.at[q, slot],
-            raw_send.at[q, n],
-            raw_recv.at[q, slot],
+            raw_send.at[min(n // (parts - 1), 1)],
+            raw_recv.at[q],
             who,
         )
 
     def mask_copy(n):
         return send(
-            mask_ref, masks.at[place], mask_sems.at[0, n], mask_sems.at[1, place], base + peers[n]
+            mask_ref, masks.at[place], mask_sems.at[0], mask_sems.at[1], base + peers[n]
         )
 
     above = jnp.logical_and(place == parts - 1, row < rows - 1)
@@ -717,7 +758,7 @@
     def _():
         raw[:, parts + 1] = jnp.zeros_like(raw[:, parts + 1])
 
-    line = Line(row, rows, lambda i: i * parts + place, HOP, (*line_buf, line_sems))
+    line = Chain(row, rows, lambda i: i * parts + place, HOP, (*line_buf, line_sems))
     line.clear()
     build_bank(bank_ref, toep)
     build_band(band)
@@ -725,19 +766,18 @@
     power[:, :LANES] = edge
     power[:, (cuts + 1) * LANES :] = edge
 
-    for b in range(parts):
-
-        @pl.when(place != b)
-        def _(b=b):
-            send(mask_ref, masks.at[b], mask_sems.at[0, 0], mask_sems.at[1, b], partner).wait_recv()
-
+    def whole(ref, send_sem, recv_sem):
+        return send(ref, ref, send_sem, recv_sem, partner)
+
+    whole(masks.at[: parts - 1], mask_sems.at[0], mask_sems.at[1]).wait_recv()
     build_pick(base, place, owner_ref, offset_ref, masks, pick)
 
+    some = back.at[:, : parts - 1]
     count = line.count
     last = HOP * (rows - 1)
 
     def give(src, dst, n, k, who):
-        return send(src.at[k], dst.at[k], give_sems.at[0, n, k], give_sems.at[1, n, k], who)
+        return send(src.at[k], dst, give_sems.at[n], give_recv.at[(n + 1) // 2, k], who)
 
     def put(k, j, value):
         src_ref[k, j] = value.astype(f32) * (1.0 / wins)
@@ -750,90 +790,109 @@
         def _():
             total = line.result(k)
             done[k] = total
-            give(done, across, 0, k, alike).start()
-            give(done, beside.at[0], 1, k, partner).start()
+            give(done, across.at[k], 0, k, alike).start()
+            give(done, beside.at[k, 0], 1, k, partner).start()
             put(k, place, total)
 
-        q = t - last - HOP
+        q = t - last - SIDE
 
         @pl.when(jnp.logical_and(q >= 0, q < count))
         def _():
-            give(done, across, 0, q, alike).wait_recv()
-            give(across, beside.at[1], 2, q, partner).start()
+            give(done, across.at[q], 0, q, alike).wait_recv()
+            give(across, beside.at[q, 1], 2, q, partner).start()
             put(q, alike_place, across[q])
 
-        b = t - last - 2 * HOP
+        b = t - last - SIDE - NEAR
 
         @pl.when(jnp.logical_and(b >= 0, b < count))
         def _():
-            give(done, beside.at[0], 1, b, partner).wait_recv()
-            put(b, partner_place, beside[0, b])
-            give(across, beside.at[1], 2, b, partner).wait_recv()
-            put(b, corner_place, beside[1, b])
+            whole(beside.at[b], give_sems.at[1], give_recv.at[1, b]).wait_recv()
+            put(b, partner_place, beside[b, 0])
+            put(b, corner_place, beside[b, 1])
+
+        @pl.when(b == 0)
+        def _():
+            whole(some, back_sems.at[0], back_sems.at[1]).wait_recv()
+            loc_ref[...] = back[...]
+
+        r = b % rounds
+
+        @pl.when(jnp.logical_and(jnp.logical_and(b >= 0, b < count), r < rounds - 1))
+        def _():
+            at = b // rounds
+            cut = pl.ds(pl.multiple_of(at * LANES, LANES), LANES)
+            loc = [[back[at, w, p] for w in range(wins)] for p in range(2)]
+
+            def wide(w, p, j):
+                return src_ref[b, w, p, pl.ds(j, 1), :]
+
+            def keep(j, real, imag):
+                part_ref[0, r * chans + j, :, cut] = real
+                part_ref[1, r * chans + j, :, cut] = imag
+
+            products(wide, loc, keep, chans)
 
     def back_copy(q, n):
         return send(
             mine.at[q, peers[n]],
             back.at[q, place],
-            back_sems.at[0, q, n],
-            back_sems.at[1, q, place],
+            back_sems.at[0],
+            back_sems.at[1],
             base + peers[n],
         )
+
+    def pass_on(q):
+        back[q, place] = mine[q, place]
+
+        @pl.loop(q * rounds, (q + 1) * rounds)
+        def _(t):
+            if last < count:
+                tick(t)
+            else:
+                line.tick(t)
+
+        for n in range(parts - 1):
+            back_copy(q, n).start()
 
     def finish(q):
         whiten_cut(q, band, pick, filt, power, line.own, mine)
-        back[q, place] = mine[q, place]
-
-        @pl.loop(q * rounds, (q + 1) * rounds)
-        def _(t):
-            tick(t)
-
-        for n in range(parts - 1):
-            back_copy(q, n).start()
-
-    for q in range(cuts):
-        for slot in range(parts + 2):
-            there = place != slot - 1
-            if slot == 0:
-                there = row > 0
-            if slot == parts + 1:
-                there = row < rows - 1
-
-            @pl.when(there)
-            def _(slot=slot, q=q):
-                raw_copy(q, 0, slot, 0, partner).wait_recv()
-
-        filter_cut(q, nbank, raw, toep, index_ref, filt, power)
-        if q > 0:
-            finish(q - 1)
-    finish(cuts - 1)
-
-    @pl.loop(cuts * rounds, count + last + 2 * HOP)
+        pass_on(q)
+
+    inner = jnp.logical_and(row > 0, row < rows - 1)
+    outer = jnp.logical_or(row == 0, row == rows - 1)
+    half = cuts // 2
+    for first in (0, half):
+        for q in range(first, first + half):
+            for there, many in ((inner, parts + 1), (outer, parts)):
+
+                @pl.when(there)
+                def _(q=q, many=many):
+                    whole(raw.at[q, :many], raw_send.at[0], raw_recv.at[q]).wait_recv()
+
+        filter_cuts(first, half, nbank, raw, toep, index_ref, filt, power)
+        if first == 0:
+            for q in range(half - 1):
+                finish(q)
+    for q in range(half - 1, cuts):
+        whiten_cut(q, band, pick, filt, power, line.own, mine)
+    for q in range(half - 1, cuts):
+        pass_on(q)
+
+    @pl.loop(cuts * rounds, count + last + SIDE + NEAR)
     def _(t):
         tick(t)
 
-    for q in range(cuts):
-        for n in range(parts - 1):
-            j = peers[n]
-            send(
-                mine.at[q, 0], back.at[q, j], back_sems.at[0, q, n], back_sems.at[1, q, j], partner
-            ).wait_recv()
-    loc_ref[...] = back[...]
-
-    for n in range(parts - 1):
-        mask_copy(n).wait_send()
-    for q in range(cuts):
-        for n in range(parts - 1):
-            raw_copy(q, peers[n], 1 + place, n, base + peers[n]).wait_send()
-            back_copy(q, n).wait_send()
-        edges(q, lambda copy: copy.wait_send())
-    line.drain()
-
-    @pl.loop(0, count)
-    def _(k):
-        give(done, across, 0, k, alike).wait_send()
-        give(done, beside.at[0], 1, k, partner).wait_send()
-        give(across, beside.at[1], 2, k, partner).wait_send()
+    whole(some, back_sems.at[0], back_sems.at[1]).wait_send()
+    whole(masks.at[: parts - 1], mask_sems.at[0], mask_sems.at[1]).wait_send()
+    whole(raw.at[:, : parts - 1], raw_send.at[0], raw_recv.at[0]).wait_send()
+
+    @pl.when(jnp.logical_or(above, below))
+    def _():
+        whole(raw.at[:, :parts], raw_send.at[1], raw_recv.at[0]).wait_send()
+
+    line.drain(partner)
+    for n in range(3):
+        whole(done, give_sems.at[n], give_recv.at[0, 0]).wait_send()
 
 
 def row_front(rows, owner, own, bank, index, mask, offset):
@@ -850,18 +909,19 @@
     return pl.pallas_call(
         functools.partial(row_kernel, rows),
         out_shape=[
-            jax.ShapeDtypeStruct((cuts, wins, *chunk), bf16),
-            jax.ShapeDtypeStruct((count, wins, *chunk), f32),
+            pltpu.VMEM((cuts, wins, *chunk), bf16),
+            pltpu.VMEM((count, wins, *chunk), f32),
+            pltpu.VMEM((2, (rounds - 1) * chans, chans, bins), bf16),
         ],
         in_specs=[pl.BlockSpec(memory_space=pltpu.HBM)] * 6,
-        out_specs=[vmem] * 2,
+        out_specs=[vmem] * 3,
         scratch_shapes=[
             pltpu.SMEM(owner.shape, owner.dtype),
             *[pltpu.VMEM(a.shape, a.dtype) for a in (own, bank, index, mask, offset)],
             pltpu.SemaphoreType.DMA((6,)),
             pltpu.VMEM((cuts, parts + 2, *chunk), bf16),
             pltpu.VMEM((parts, wins, chans), jnp.int32),
-            pltpu.VMEM((2, nbank * 2 * outs, 2 * LANES), bf16),
+            pltpu.VMEM((nbank * 2 * outs, 4 * LANES), bf16),
             pltpu.VMEM((3 * LANES, LANES), bf16),
             pltpu.VMEM(((rounds + parts) * chans, parts * chans), bf16),
             pltpu.VMEM((cuts, 2, parts * chans, LANES), f32),
@@ -871,13 +931,14 @@
             [chunks] * 5,
             chunks,
             chunks,
-            pltpu.VMEM((2, count, *chunk), bf16),
-            pltpu.SemaphoreType.DMA((cuts, 2 * parts - 1)),
-            pltpu.SemaphoreType.DMA((cuts, parts + 2)),
-            pltpu.SemaphoreType.DMA((2, parts)),
-            pltpu.SemaphoreType.DMA((2, cuts, parts)),
-            pltpu.SemaphoreType.DMA((2, 2, count)),
-            pltpu.SemaphoreType.DMA((2, 3, count)),
+            pltpu.VMEM((count, 2, *chunk), bf16),
+            pltpu.SemaphoreType.DMA((2,)),
+            pltpu.SemaphoreType.DMA((cuts,)),
+            pltpu.SemaphoreType.DMA((2,)),
+            pltpu.SemaphoreType.DMA((2,)),
+            pltpu.SemaphoreType.DMA((2, count + 1)),
+            pltpu.SemaphoreType.DMA((3,)),
+            pltpu.SemaphoreType.DMA((2, count)),
         ],
         compiler_params=pltpu.CompilerParams(
             collective_id=0, has_side_effects=True, vmem_limit_bytes=24 << 20
@@ -886,74 +947,82 @@
     )(*[pltpu.with_memory_space_constraint(a, pltpu.HBM) for a in (owner, own, bank, index, mask, offset)])
 
 
-def pairs_kernel(src_ref, loc_ref, out_ref, buf, sems):
+def products(wide, loc, put, count):
+    wins = len(loc[0])
+    chans = loc[0][0].shape[0]
+
+    def one(j, carry):
+        src = [
+            [
+                jnp.broadcast_to(wide(w, p, j), (chans, LANES)).astype(bf16)
+                for w in range(wins)
+            ]
+            for p in range(2)
+        ]
+        real = tree_sum([src[p][w] * loc[p][w] for w in range(wins) for p in range(2)])
+        plus = tree_sum([src[0][w] * loc[1][w] for w in range(wins)])
+        minus = tree_sum([src[1][w] * loc[0][w] for w in range(wins)])
+        put(j, real, plus - minus)
+        return carry
+
+    lax.fori_loop(0, count, one, 0, unroll=8)
+
+
+def pairs_kernel(src_ref, loc_ref, part_ref, out_ref, buf, sems):
     cuts, wins, _, chans, _ = loc_ref.shape
-    slots, _, per = buf.shape[:3]
+    steps, _, per = buf.shape[:3]
     rounds = src_ref.shape[0] // cuts
-    steps = rounds * chans // per
-
-    def flush(step):
-        slot = step % slots
+    ready = rounds - 1
+
+    def flush(r):
+        rows = slice(r * chans, (r + 1) * chans)
+        return pltpu.make_async_copy(part_ref.at[:, rows], out_ref.at[:, rows], sems.at[r])
+
+    def last(step):
+        at = ready * chans + step * per
         return pltpu.make_async_copy(
-            buf.at[slot], out_ref.at[:, pl.ds(step * per, per)], sems.at[slot]
-        )
-
-    @pl.loop(0, steps)
-    def _(step):
-        slot = step % slots
-        r = step * per // chans
-        first = step * per % chans
-
-        @pl.when(step >= slots)
-        def _():
-            flush(step - slots).wait()
-
+            buf.at[step], out_ref.at[:, at : at + per], sems.at[ready + step]
+        )
+
+    for r in range(ready):
+        flush(r).start()
+    for step in range(steps):
         for q in range(cuts):
             loc = [[loc_ref[q, w, p] for w in range(wins)] for p in range(2)]
 
-            def one(j, carry, q=q, loc=loc):
-                src = [
-                    [
-                        jnp.broadcast_to(
-                            src_ref[q * rounds + r, w, p, pl.ds(first + j, 1), :], (chans, LANES)
-                        ).astype(bf16)
-                        for w in range(wins)
-                    ]
-                    for p in range(2)
-                ]
-                real = tree_sum([src[p][w] * loc[p][w] for w in range(wins) for p in range(2)])
-                plus = tree_sum([src[0][w] * loc[1][w] for w in range(wins)])
-                minus = tree_sum([src[1][w] * loc[0][w] for w in range(wins)])
+            def wide(w, p, j, q=q, step=step):
+                return src_ref[q * rounds + ready, w, p, pl.ds(step * per + j, 1), :]
+
+            def put(j, real, imag, q=q, step=step):
                 cut = slice(q * LANES, (q + 1) * LANES)
-                buf[slot, 0, j, :, cut] = real
-                buf[slot, 1, j, :, cut] = plus - minus
-                return carry
-
-            lax.fori_loop(0, per, one, 0, unroll=8)
-        flush(step).start()
-
-    for n in range(slots):
-        flush(steps - slots + n).wait()
-
-
-def pairs(src, loc):
+                buf[step, 0, j, :, cut] = real
+                buf[step, 1, j, :, cut] = imag
+
+            products(wide, loc, put, per)
+        last(step).start()
+    for r in range(ready):
+        flush(r).wait()
+    for step in range(steps):
+        last(step).wait()
+
+
+def pairs(src, loc, part):
     cuts, wins, _, chans, _ = loc.shape
-    count = src.shape[0] // cuts * chans
-    per = chans // 2
-    slots = 2
+    rounds = src.shape[0] // cuts
+    steps = 2
     vmem = pl.BlockSpec(memory_space=pltpu.VMEM)
     return pl.pallas_call(
         pairs_kernel,
-        out_shape=jax.ShapeDtypeStruct((2, count, chans, cuts * LANES), bf16),
-        in_specs=[vmem] * 2,
+        out_shape=jax.ShapeDtypeStruct((2, rounds * chans, chans, cuts * LANES), bf16),
+        in_specs=[vmem] * 3,
         out_specs=pl.BlockSpec(memory_space=pl.ANY),
         scratch_shapes=[
-            pltpu.VMEM((slots, 2, per, chans, cuts * LANES), bf16),
-            pltpu.SemaphoreType.DMA((slots,)),
+            pltpu.VMEM((steps, 2, chans // steps, chans, cuts * LANES), bf16),
+            pltpu.SemaphoreType.DMA((rounds - 1 + steps,)),
         ],
         compiler_params=pltpu.CompilerParams(vmem_limit_bytes=16 << 20),
         name="pairs",
-    )(src, loc)
+    )(src, loc, part)
 
 
 def body(spectra, filter_bank, band_index, window_mask, owner_order, source_offset):
@@ -961,7 +1030,7 @@
     _, wins, chans, bins = spectra.shape
     ntap = filter_bank.shape[2]
     if 2 * grid[1] == wins == 4 and 4 * chans == LANES and ntap == 2 * chans + 1:
-        whitened, sources = row_front(
+        whitened, sources, part = row_front(
             grid[0],
             owner_order,
             spectra,
@@ -970,7 +1039,7 @@
             window_mask,
             source_offset,
         )
-        return pairs(sources, whitened)
+        return pairs(sources, whitened, part)
     whitened, sources = front(
         grid, owner_order, spectra, filter_bank, band_index[None, :], window_mask
     )

time: 39.3 us -> 33.7 us (0.86)
  Pallas kernels: 39 us -> 33.6 us
    pallas_call x2, Pallas kernels: 39 us -> 33.6 us  [the longest x1 30.2 us: row_front(): pl.pallas_call(functools.partial(row_kernel, rows), out_shape=[pltpu.VMEM...]
where the time goes in v2:
time: 33.7 us; the launch traced here: 33.6 us
  Pallas kernels  33.6 us (100%)
    pallas_call x1, Pallas kernels, row_front(): pl.pallas_call(functools.partial(row_kernel, rows), out_shape=[pltpu.VMEM...  30.2 us
    pallas_call x1, Pallas kernels, pairs(): pl.pallas_call(pairs_kernel, out_shape=jax.ShapeDtypeStruct((2, rounds *...  3.34 us

profile of v2, /device:TPU:0, one launch (start us, length us, event | category | flops | bytes accessed | tf_op | source)
XLA Modules:
  0.0 33.6 jit_solution(16520227430855483464)
XLA Ops:
  0.0 30.2 %front.1 = (bf16[4,4,2,32,128]{4,3,2,1,0:T(8,128)(2,1)S(1)}, f32[16,4,2,32,128]{4,3,2,1,0:T(8,128)S(1)}, bf16[2,96,32,512]{3,2,1,0:T(8,128)(2,1)S(1)}) custom-call(s32[4]{0:T(128)} %owner_in.1, bf16[2,4,32,512]{3,2,1,0:T(8,128)(2,1)} %own_in.1, f32[2,8,65]{2,1,0:T(8,128)} %bank_in.1, s32[1,512]{1,0:T(1,128)} %bitcast.1, s32[4,32]{1,0:T(4,128)} %mask_in.1, ...), custom_call_target="tpu_custom_call" | custom-call | tf_op jit(solution)/shard_map/front/pallas_call | solution.py:909
  30.2 3.3 %pairs.1 = bf16[2,128,32,512]{3,2,1,0:T(8,128)(2,1)} custom-call(f32[16,4,2,32,128]{4,3,2,1,0:T(8,128)S(1)} %get-tuple-element.8.src_ref, bf16[4,4,2,32,128]{4,3,2,1,0:T(8,128)(2,1)S(1)} %get-tuple-element.9.loc_ref, bf16[2,96,32,512]{3,2,1,0:T(8,128)(2,1)S(1)} %get-tuple-element.10.part_ref), custom_call_target="tpu_custom_call" | custom-call | tf_op jit(solution)/shard_map/pairs/pallas_call | solution.py:1014

commit v3 on v2

--- a/solution.py
+++ b/solution.py
@@ -479,7 +479,7 @@
     return chips // cols, cols
 
 
-HOP, SIDE, NEAR = 10, 8, 4
+HOP, SIDE, NEAR, LATE = 10, 8, 4, 7
 
 
 class Chain(Line):
@@ -566,12 +566,8 @@
     index = index_ref[:, first * LANES : (first + cuts) * LANES]
     for u in range((blocks - 2) // step):
         here = [
-            jnp.concatenate(
-                [
-                    raw[q, u * step : u * step + step + 2, p].reshape((step + 2) * chans, LANES)
-                    for q in many
-                ],
-                axis=1,
+            raw[first // cuts, u * step : u * step + step + 2, p].reshape(
+                (step + 2) * chans, cuts * LANES
             )
             for p in range(2)
         ]
@@ -649,7 +645,8 @@
     give_recv,
 ):
     wins, chans = mask_ref.shape
-    cuts = raw.shape[0]
+    halves, span = raw.shape[0], raw.shape[4]
+    cuts = halves * span // LANES
     nbank = bank_ref.shape[1]
     parts = wins
     rounds = owner_ref.shape[0]
@@ -710,7 +707,7 @@
 
     def raw_copy(q, to, slot, n, who):
         return send(
-            own_ref.at[:, to, :, q * LANES : (q + 1) * LANES],
+            own_ref.at[:, to, :, q * span : (q + 1) * span],
             raw.at[q, slot],
             raw_send.at[min(n // (parts - 1), 1)],
             raw_recv.at[q],
@@ -740,15 +737,15 @@
         copy.wait()
     for n in range(parts - 1):
         mask_copy(n).start()
-    for q in range(cuts):
+    for q in range(halves):
         for n in range(2):
             raw_copy(q, peers[n], 1 + place, n, base + peers[n]).start()
         edges(q, lambda copy: copy.start())
         raw_copy(q, peers[2], 1 + place, 2, base + peers[2]).start()
 
     masks[place] = mask_ref[...]
-    for q in range(cuts):
-        raw[q, 1 + place] = own_ref[:, place, :, q * LANES : (q + 1) * LANES]
+    for q in range(halves):
+        raw[q, 1 + place] = own_ref[:, place, :, q * span : (q + 1) * span]
 
     @pl.when(row == 0)
     def _():
@@ -815,11 +812,9 @@
             whole(some, back_sems.at[0], back_sems.at[1]).wait_recv()
             loc_ref[...] = back[...]
 
-        r = b % rounds
-
-        @pl.when(jnp.logical_and(jnp.logical_and(b >= 0, b < count), r < rounds - 1))
+        @pl.when(jnp.logical_and(b >= 0, b < count - LATE))
         def _():
-            at = b // rounds
+            at, r = b // rounds, b % rounds
             cut = pl.ds(pl.multiple_of(at * LANES, LANES), LANES)
             loc = [[back[at, w, p] for w in range(wins)] for p in range(2)]
 
@@ -860,14 +855,13 @@
 
     inner = jnp.logical_and(row > 0, row < rows - 1)
     outer = jnp.logical_or(row == 0, row == rows - 1)
-    half = cuts // 2
-    for first in (0, half):
-        for q in range(first, first + half):
-            for there, many in ((inner, parts + 1), (outer, parts)):
-
-                @pl.when(there)
-                def _(q=q, many=many):
-                    whole(raw.at[q, :many], raw_send.at[0], raw_recv.at[q]).wait_recv()
+    half = cuts // halves
+    for first in range(0, cuts, half):
+        for there, many in ((inner, parts + 1), (outer, parts)):
+
+            @pl.when(there)
+            def _(q=first // half, many=many):
+                whole(raw.at[q, :many], raw_send.at[0], raw_recv.at[q]).wait_recv()
 
         filter_cuts(first, half, nbank, raw, toep, index_ref, filt, power)
         if first == 0:
@@ -911,7 +905,7 @@
         out_shape=[
             pltpu.VMEM((cuts, wins, *chunk), bf16),
             pltpu.VMEM((count, wins, *chunk), f32),
-            pltpu.VMEM((2, (rounds - 1) * chans, chans, bins), bf16),
+            pltpu.VMEM((2, rounds * chans, chans, bins), bf16),
         ],
         in_specs=[pl.BlockSpec(memory_space=pltpu.HBM)] * 6,
         out_specs=[vmem] * 3,
@@ -919,7 +913,7 @@
             pltpu.SMEM(owner.shape, owner.dtype),
             *[pltpu.VMEM(a.shape, a.dtype) for a in (own, bank, index, mask, offset)],
             pltpu.SemaphoreType.DMA((6,)),
-            pltpu.VMEM((cuts, parts + 2, *chunk), bf16),
+            pltpu.VMEM((2, parts + 2, 2, chans, bins // 2), bf16),
             pltpu.VMEM((parts, wins, chans), jnp.int32),
             pltpu.VMEM((nbank * 2 * outs, 4 * LANES), bf16),
             pltpu.VMEM((3 * LANES, LANES), bf16),
@@ -933,7 +927,7 @@
             chunks,
             pltpu.VMEM((count, 2, *chunk), bf16),
             pltpu.SemaphoreType.DMA((2,)),
-            pltpu.SemaphoreType.DMA((cuts,)),
+            pltpu.SemaphoreType.DMA((2,)),
             pltpu.SemaphoreType.DMA((2,)),
             pltpu.SemaphoreType.DMA((2,)),
             pltpu.SemaphoreType.DMA((2, count + 1)),
@@ -965,60 +959,61 @@
         put(j, real, plus - minus)
         return carry
 
-    lax.fori_loop(0, count, one, 0, unroll=8)
+    lax.fori_loop(0, count, one, 0, unroll=16)
 
 
 def pairs_kernel(src_ref, loc_ref, part_ref, out_ref, buf, sems):
     cuts, wins, _, chans, _ = loc_ref.shape
-    steps, _, per = buf.shape[:3]
-    rounds = src_ref.shape[0] // cuts
-    ready = rounds - 1
-
-    def flush(r):
-        rows = slice(r * chans, (r + 1) * chans)
-        return pltpu.make_async_copy(part_ref.at[:, rows], out_ref.at[:, rows], sems.at[r])
-
-    def last(step):
-        at = ready * chans + step * per
-        return pltpu.make_async_copy(
-            buf.at[step], out_ref.at[:, at : at + per], sems.at[ready + step]
-        )
-
-    for r in range(ready):
-        flush(r).start()
-    for step in range(steps):
-        for q in range(cuts):
-            loc = [[loc_ref[q, w, p] for w in range(wins)] for p in range(2)]
-
-            def wide(w, p, j, q=q, step=step):
-                return src_ref[q * rounds + ready, w, p, pl.ds(step * per + j, 1), :]
-
-            def put(j, real, imag, q=q, step=step):
-                cut = slice(q * LANES, (q + 1) * LANES)
-                buf[step, 0, j, :, cut] = real
-                buf[step, 1, j, :, cut] = imag
-
-            products(wide, loc, put, per)
-        last(step).start()
-    for r in range(ready):
-        flush(r).wait()
-    for step in range(steps):
-        last(step).wait()
+    count = src_ref.shape[0]
+    rounds = count // cuts
+    first = count - buf.shape[0]
+
+    def place_of(k, many=1):
+        q, r = k // rounds, k % rounds
+        rows = slice(r * chans, (r + many) * chans)
+        return (slice(None), rows, slice(None), slice(q * LANES, (q + 1) * LANES))
+
+    copies = []
+    for k in range(0, first, rounds):
+        at = place_of(k, min(rounds, first - k))
+        copies.append(
+            pltpu.make_async_copy(part_ref.at[at], out_ref.at[at], sems.at[len(copies)])
+        )
+        copies[-1].start()
+    for k in range(first, count):
+        loc = [[loc_ref[k // rounds, w, p] for w in range(wins)] for p in range(2)]
+
+        def wide(w, p, j, k=k):
+            return src_ref[k, w, p, pl.ds(j, 1), :]
+
+        def put(j, real, imag, k=k):
+            buf[k - first, 0, j] = real
+            buf[k - first, 1, j] = imag
+
+        products(wide, loc, put, chans)
+        copies.append(
+            pltpu.make_async_copy(
+                buf.at[k - first], out_ref.at[place_of(k)], sems.at[len(copies)]
+            )
+        )
+        copies[-1].start()
+    for copy in copies:
+        copy.wait()
 
 
 def pairs(src, loc, part):
-    cuts, wins, _, chans, _ = loc.shape
-    rounds = src.shape[0] // cuts
-    steps = 2
+    cuts, _, _, chans, _ = loc.shape
+    count = src.shape[0]
+    late = min(LATE, count)
     vmem = pl.BlockSpec(memory_space=pltpu.VMEM)
     return pl.pallas_call(
         pairs_kernel,
-        out_shape=jax.ShapeDtypeStruct((2, rounds * chans, chans, cuts * LANES), bf16),
+        out_shape=jax.ShapeDtypeStruct(part.shape, bf16),
         in_specs=[vmem] * 3,
         out_specs=pl.BlockSpec(memory_space=pl.ANY),
         scratch_shapes=[
-            pltpu.VMEM((steps, 2, chans // steps, chans, cuts * LANES), bf16),
-            pltpu.SemaphoreType.DMA((rounds - 1 + steps,)),
+            pltpu.VMEM((late, 2, chans, chans, LANES), bf16),
+            pltpu.SemaphoreType.DMA((cuts + late,)),
         ],
         compiler_params=pltpu.CompilerParams(vmem_limit_bytes=16 << 20),
         name="pairs",

time: 33.7 us -> 32.3 us (0.958)
  Pallas kernels: 33.6 us -> 32.1 us
    pallas_call x1, Pallas kernels: 30.2 us -> 28.7 us  [row_front(): pl.pallas_call(functools.partial(row_kernel, rows), out_shape=[pltpu.VMEM...]
where the time goes in v3:
time: 32.3 us; the launch traced here: 32.1 us
  Pallas kernels  32.1 us (99%)
    pallas_call x1, Pallas kernels, row_front(): pl.pallas_call(functools.partial(row_kernel, rows), out_shape=[pltpu.VMEM...  28.7 us
    pallas_call x1, Pallas kernels, pairs(): pl.pallas_call(pairs_kernel, out_shape=jax.ShapeDtypeStruct(part.shape, b...  3.45 us

profile of v3, /device:TPU:0, one launch (start us, length us, event | category | flops | bytes accessed | tf_op | source)
XLA Modules:
  0.0 32.1 jit_solution(190301338940683944)
XLA Ops:
  0.0 28.7 %front.1 = (bf16[4,4,2,32,128]{4,3,2,1,0:T(8,128)(2,1)S(1)}, f32[16,4,2,32,128]{4,3,2,1,0:T(8,128)S(1)}, bf16[2,128,32,512]{3,2,1,0:T(8,128)(2,1)S(1)}) custom-call(s32[4]{0:T(128)} %owner_in.1, bf16[2,4,32,512]{3,2,1,0:T(8,128)(2,1)} %own_in.1, f32[2,8,65]{2,1,0:T(8,128)} %bank_in.1, s32[1,512]{1,0:T(1,128)} %bitcast.1, s32[4,32]{1,0:T(4,128)} %mask_in.1, ...), custom_call_target="tpu_custom_call" | custom-call | tf_op jit(solution)/shard_map/front/pallas_call | solution.py:903
  28.7 3.5 %pairs.1 = bf16[2,128,32,512]{3,2,1,0:T(8,128)(2,1)} custom-call(f32[16,4,2,32,128]{4,3,2,1,0:T(8,128)S(1)} %get-tuple-element.8.src_ref, bf16[4,4,2,32,128]{4,3,2,1,0:T(8,128)(2,1)S(1)} %get-tuple-element.9.loc_ref, bf16[2,128,32,512]{3,2,1,0:T(8,128)(2,1)S(1)} %get-tuple-element.10.part_ref), custom_call_target="tpu_custom_call" | custom-call | tf_op jit(solution)/shard_map/pairs/pallas_call | solution.py:1009

commit v4 on v3

--- a/solution.py
+++ b/solution.py
@@ -479,7 +479,7 @@
     return chips // cols, cols
 
 
-HOP, SIDE, NEAR, LATE = 10, 8, 4, 7
+HOP, SIDE, NEAR, LATE = 8, 8, 4, 7
 
 
 class Chain(Line):
@@ -595,14 +595,15 @@
         power[:, q * LANES : (q + 3) * LANES], band[...], preferred_element_type=f32
     )
     scale = lax.rsqrt(smooth * (1.0 / SMOOTH) + water_level)
+    white = jnp.concatenate([(filt[q, p] * scale).astype(bf16) for p in range(2)], axis=1)
+    res = jnp.dot(pick[...], white, preferred_element_type=f32).astype(bf16)
+    at = rounds * chans
     for p in range(2):
-        white = (filt[q, p] * scale).astype(bf16)
-        res = jnp.dot(pick[...], white, preferred_element_type=f32).astype(bf16)
+        cut = slice(p * LANES, (p + 1) * LANES)
         for r in range(rounds):
-            own[q * rounds + r, p] = res[r * chans : (r + 1) * chans]
-        at = rounds * chans
+            own[q * rounds + r, p] = res[r * chans : (r + 1) * chans, cut]
         for b in range(mine.shape[1]):
-            mine[q, b, p] = res[at + b * chans : at + (b + 1) * chans]
+            mine[q, b, p] = res[at + b * chans : at + (b + 1) * chans, cut]
 
 
 def row_kernel(
@@ -959,7 +960,7 @@
         put(j, real, plus - minus)
         return carry
 
-    lax.fori_loop(0, count, one, 0, unroll=16)
+    lax.fori_loop(0, count, one, 0, unroll=32)
 
 
 def pairs_kernel(src_ref, loc_ref, part_ref, out_ref, buf, sems):

time: 32.3 us -> 31.9 us (0.988)
  no operation moved by 1% of the time
where the time goes in v4:
time: 31.9 us; the launch traced here: 31.8 us
  Pallas kernels  31.8 us (100%)
    pallas_call x1, Pallas kernels, row_front(): pl.pallas_call(functools.partial(row_kernel, rows), out_shape=[pltpu.VMEM...  28.4 us
    pallas_call x1, Pallas kernels, pairs(): pl.pallas_call(pairs_kernel, out_shape=jax.ShapeDtypeStruct(part.shape, b...  3.37 us

profile of v4, /device:TPU:0, one launch (start us, length us, event | category | flops | bytes accessed | tf_op | source)
XLA Modules:
  0.0 31.8 jit_solution(10484619012631602091)
XLA Ops:
  0.0 28.4 %front.1 = (bf16[4,4,2,32,128]{4,3,2,1,0:T(8,128)(2,1)S(1)}, f32[16,4,2,32,128]{4,3,2,1,0:T(8,128)S(1)}, bf16[2,128,32,512]{3,2,1,0:T(8,128)(2,1)S(1)}) custom-call(s32[4]{0:T(128)} %owner_in.1, bf16[2,4,32,512]{3,2,1,0:T(8,128)(2,1)} %own_in.1, f32[2,8,65]{2,1,0:T(8,128)} %bank_in.1, s32[1,512]{1,0:T(1,128)} %bitcast.1, s32[4,32]{1,0:T(4,128)} %mask_in.1, ...), custom_call_target="tpu_custom_call" | custom-call | tf_op jit(solution)/shard_map/front/pallas_call | solution.py:904
  28.4 3.4 %pairs.1 = bf16[2,128,32,512]{3,2,1,0:T(8,128)(2,1)} custom-call(f32[16,4,2,32,128]{4,3,2,1,0:T(8,128)S(1)} %get-tuple-element.8.src_ref, bf16[4,4,2,32,128]{4,3,2,1,0:T(8,128)(2,1)S(1)} %get-tuple-element.9.loc_ref, bf16[2,128,32,512]{3,2,1,0:T(8,128)(2,1)S(1)} %get-tuple-element.10.part_ref), custom_call_target="tpu_custom_call" | custom-call | tf_op jit(solution)/shard_map/pairs/pallas_call | solution.py:1010

commit v5 on v4

--- a/solution.py
+++ b/solution.py
@@ -479,7 +479,7 @@
     return chips // cols, cols
 
 
-HOP, SIDE, NEAR, LATE = 8, 8, 4, 7
+UP, DOWN, SIDE, NEAR, LATE = 8, 8, 8, 4, 7
 
 
 class Chain(Line):
@@ -497,6 +497,22 @@
             device_id={"chan": who},
             device_id_type=pl.DeviceIdType.MESH,
         )
+
+    def tick(self, t):
+        for way in (1, 0):
+            behind = self.pos if way == 0 else self.length - 1 - self.pos
+            out, into = (self.out_r, self.in_r) if way == 0 else (self.out_l, self.in_l)
+            k = t - self.lag[way] * behind
+            inside = jnp.logical_and(k >= 0, k < self.count)
+
+            @pl.when(jnp.logical_and(inside, behind > 0))
+            def _(way=way, k=k):
+                self.copy(way, k).wait_recv()
+
+            @pl.when(jnp.logical_and(inside, behind < self.length - 1))
+            def _(way=way, k=k, out=out, into=into):
+                out[k] = self.own[k] + into[k]
+                self.copy(way, k).start()
 
     def drain(self, who):
         for way in range(2):
@@ -552,7 +568,7 @@
         row = jnp.broadcast_to(offset_ref[r : r + 1, :].astype(f32), (chans, chans))
         col = jnp.sum(jnp.where(eye, row, 0.0), axis=1, keepdims=True)
         col = col + ((owner_ref[r] - base) * chans).astype(f32)
-        pick[r * chans : (r + 1) * chans] = jnp.where(cols == col, valid, 0.0).astype(bf16)
+        pick[r * chans : (r + 1) * chans] = jnp.where(cols == col, valid * (1.0 / parts), 0.0).astype(bf16)
     rows = lax.broadcasted_iota(jnp.int32, (total, total), 0)
     same = rows == lax.broadcasted_iota(jnp.int32, (total, total), 1)
     pick[rounds * chans :] = jnp.where(same, valid, 0.0).astype(bf16)
@@ -756,7 +772,7 @@
     def _():
         raw[:, parts + 1] = jnp.zeros_like(raw[:, parts + 1])
 
-    line = Chain(row, rows, lambda i: i * parts + place, HOP, (*line_buf, line_sems))
+    line = Chain(row, rows, lambda i: i * parts + place, (UP, DOWN), (*line_buf, line_sems))
     line.clear()
     build_bank(bank_ref, toep)
     build_band(band)
@@ -772,13 +788,14 @@
 
     some = back.at[:, : parts - 1]
     count = line.count
-    last = HOP * (rows - 1)
+    last = jnp.maximum(jnp.maximum(UP * row, DOWN * (rows - 1 - row)), count)
+    longest = max(max(UP, DOWN) * (rows - 1), count)
 
     def give(src, dst, n, k, who):
         return send(src.at[k], dst, give_sems.at[n], give_recv.at[(n + 1) // 2, k], who)
 
     def put(k, j, value):
-        src_ref[k, j] = value.astype(f32) * (1.0 / wins)
+        src_ref[k, j] = value.astype(f32)
 
     def tick(t):
         line.tick(t)
@@ -842,10 +859,7 @@
 
         @pl.loop(q * rounds, (q + 1) * rounds)
         def _(t):
-            if last < count:
-                tick(t)
-            else:
-                line.tick(t)
+            line.tick(t)
 
         for n in range(parts - 1):
             back_copy(q, n).start()
@@ -873,7 +887,7 @@
     for q in range(half - 1, cuts):
         pass_on(q)
 
-    @pl.loop(cuts * rounds, count + last + SIDE + NEAR)
+    @pl.loop(cuts * rounds, count + longest + SIDE + NEAR)
     def _(t):
         tick(t)
 

time: 31.9 us -> 32 us (level)
  no operation moved by 1% of the time
where the time goes in v5:
time: 32 us; the launch traced here: 31.8 us
  Pallas kernels  31.8 us (99%)
    pallas_call x1, Pallas kernels, row_front(): pl.pallas_call(functools.partial(row_kernel, rows), out_shape=[pltpu.VMEM...  28.4 us
    pallas_call x1, Pallas kernels, pairs(): pl.pallas_call(pairs_kernel, out_shape=jax.ShapeDtypeStruct(part.shape, b...  3.37 us

profile of v5, /device:TPU:0, one launch (start us, length us, event | category | flops | bytes accessed | tf_op | source)
XLA Modules:
  0.0 31.8 jit_solution(3442788669023375395)
XLA Ops:
  0.0 28.4 %front.1 = (bf16[4,4,2,32,128]{4,3,2,1,0:T(8,128)(2,1)S(1)}, f32[16,4,2,32,128]{4,3,2,1,0:T(8,128)S(1)}, bf16[2,128,32,512]{3,2,1,0:T(8,128)(2,1)S(1)}) custom-call(s32[4]{0:T(128)} %owner_in.1, bf16[2,4,32,512]{3,2,1,0:T(8,128)(2,1)} %own_in.1, f32[2,8,65]{2,1,0:T(8,128)} %bank_in.1, s32[1,512]{1,0:T(1,128)} %bitcast.1, s32[4,32]{1,0:T(4,128)} %mask_in.1, ...), custom_call_target="tpu_custom_call" | custom-call | tf_op jit(solution)/shard_map/front/pallas_call | solution.py:918
  28.5 3.4 %pairs.1 = bf16[2,128,32,512]{3,2,1,0:T(8,128)(2,1)} custom-call(f32[16,4,2,32,128]{4,3,2,1,0:T(8,128)S(1)} %get-tuple-element.8.src_ref, bf16[4,4,2,32,128]{4,3,2,1,0:T(8,128)(2,1)S(1)} %get-tuple-element.9.loc_ref, bf16[2,128,32,512]{3,2,1,0:T(8,128)(2,1)S(1)} %get-tuple-element.10.part_ref), custom_call_target="tpu_custom_call" | custom-call | tf_op jit(solution)/shard_map/pairs/pallas_call | solution.py:1024
